TPU v7x, 32 devices: a whole 2x2x4 slice. The times are simulated.
32 devices in a mesh: row: 2 (over x), col: 4 (over y, core), mode: 4 (over z).
Axes of the slice: x: 2, y: 2, z: 4, core: 2. Of those that a mesh axis runs over, the one named last changes fastest.
Arguments:
- object_field: float32 [2, 512, 1024], P(None, 'row', 'col'), may hold values from -6 to 6
- probe_real: float32 [4, 128, 128], P('mode'), may hold values from -3 to 3
- probe_imag: float32 [4, 128, 128], P('mode'), may hold values from -3 to 3
- amplitude: float32 [2, 4, 8, 128, 128], P('row', 'col'), may hold values from 0 to 3
- positions: int32 [2, 4, 8, 2], P('row', 'col'), may hold values from 0 to 256, as said below
- counts: int32 [2, 4], P('row', 'col'), may hold values from 2 to 8, as said below
Outputs:
- updated: float32 [2, 512, 1024], P(None, 'row', 'col')
Inputs may be any that keep to these rules, and one draw needn't show every extreme that they name: `positions`: offsets lie in 0 to 256 for rows and 0 to 256 for columns. In every tile slot 0 starts within the first 64 rows and columns of the window, and slot 1 ends within the last 64 rows and columns. `counts`: some tile has 8 frames and some tile has 2.
All inputs are finite; a program needn't handle non-finite values.
Results may differ from a plain program's by a relative error of at most 0.0003.
Values sent between devices are 32-bit elements; how exact they have to be, the bound alone decides.
A program may use at most 64 MiB of HBM per device.

v0:
```python
from functools import partial
import jax
import jax.numpy as jnp
from jax import lax
from jax.sharding import PartitionSpec as P

FRAME = 128
MARGIN = 64
SLOTS = 8
STEP_SIZE = 0.25


def padded(cells, sides, width):
    for axis, dim in sides:
        count = lax.axis_size(axis)
        ends = count - 1
        head = lax.slice_in_dim(cells, 0, width, axis=dim)
        tail = lax.slice_in_dim(cells, cells.shape[dim] - width, cells.shape[dim], axis=dim)
        cells = jnp.concatenate(
            [
                lax.ppermute(tail, axis, [(i, (i + 1) % count) for i in range(ends)]),
                cells,
                lax.ppermute(head, axis, [((i + 1) % count, i) for i in range(ends)]),
            ],
            axis=dim,
        )
    return cells


def tables(length):
    counter = jnp.arange(length, dtype=jnp.int32)
    phase = counter[:, None] * counter[None, :] % length
    angles = phase.astype(jnp.float32) * (2.0 * jnp.pi / length)
    factor = 1.0 / jnp.sqrt(jnp.float32(length))
    return (jnp.cos(angles) * factor, jnp.sin(angles) * factor)


def transform(real_part, imag_part, cosine, sine_table, direction):
    product = partial(jnp.matmul, precision=lax.Precision.HIGHEST)
    left_real = product(cosine, real_part) + direction * product(sine_table, imag_part)
    left_imag = product(cosine, imag_part) - direction * product(sine_table, real_part)
    out_real = product(left_real, cosine) + direction * product(left_imag, sine_table)
    out_imag = product(left_imag, cosine) - direction * product(left_real, sine_table)
    return (out_real, out_imag)


def forward_wave(window, mode_real, mode_imag, cosine, sine_table):
    object_real = window[..., 0, :, :]
    object_imag = window[..., 1, :, :]
    wave_real = mode_real * object_real - mode_imag * object_imag
    wave_imag = mode_real * object_imag + mode_imag * object_real
    return transform(wave_real, wave_imag, cosine, sine_table, 1.0)


def backward_wave(
    spec_real, spec_imag, intensity, target, mode_real, mode_imag, cosine, sine_table
):
    keep = 1.0 - target / jnp.maximum(jnp.sqrt(intensity), 1.0)
    back_real, back_imag = transform(spec_real * keep, spec_imag * keep, cosine, sine_table, -1.0)
    grad_real = mode_real * back_real + mode_imag * back_imag
    grad_imag = mode_real * back_imag - mode_imag * back_real
    return jnp.stack([grad_real, grad_imag], axis=-3)


def fold_rims(gradient):
    margin = MARGIN
    borders = jnp.concatenate([gradient[:, :margin], gradient[:, -margin:]], axis=1)
    received = padded(borders, (("row", 1),), margin)
    interior = gradient[:, margin:-margin]
    interior = interior.at[:, :margin].add(received[:, :margin])
    interior = interior.at[:, -margin:].add(received[:, -margin:])
    sideways = jnp.concatenate([interior[:, :, :margin], interior[:, :, -margin:]], axis=2)
    arrived = padded(sideways, (("col", 2),), margin)
    centre = interior[:, :, margin:-margin]
    centre = centre.at[:, :, :margin].add(arrived[:, :, :margin])
    centre = centre.at[:, :, -margin:].add(arrived[:, :, -margin:])
    return centre


def per_device(object_field, probe_real, probe_imag, amplitude, positions, counts):
    cosine, sine_table = tables(FRAME)
    extended = padded(object_field, (("row", 1), ("col", 2)), MARGIN)
    measured = amplitude[0, 0]
    offsets = positions[0, 0]
    active = counts[0, 0]
    anchor = jnp.zeros((), jnp.int32)

    def window_of(slot):
        return lax.dynamic_slice(
            extended, (anchor, offsets[slot, 0], offsets[slot, 1]), (2, FRAME, FRAME)
        )

    def deposit(gradient, slot, contrib):
        weight = (slot < active).astype(jnp.float32)
        corner = (anchor, offsets[slot, 0], offsets[slot, 1])
        previous = lax.dynamic_slice(gradient, corner, (2, FRAME, FRAME))
        return lax.dynamic_update_slice(gradient, previous + contrib * weight, corner)

    gradient = jnp.zeros(extended.shape, jnp.float32)
    all_real, all_imag = (
        lax.all_gather(probe_real, "mode", axis=0, tiled=True),
        lax.all_gather(probe_imag, "mode", axis=0, tiled=True),
    )
    member = lax.axis_index("mode")
    group = lax.axis_size("mode")

    def advance_own(turn, gradient):
        slot = member + turn * group
        spec_real, spec_imag = forward_wave(window_of(slot), all_real, all_imag, cosine, sine_table)
        intensity = jnp.sum(spec_real * spec_real + spec_imag * spec_imag, axis=0)
        terms = backward_wave(
            spec_real, spec_imag, intensity, measured[slot], all_real, all_imag, cosine, sine_table
        )
        return deposit(gradient, slot, jnp.sum(terms, axis=0))

    gradient = lax.fori_loop(0, SLOTS // group, advance_own, gradient)
    summed = lax.psum(gradient, "mode")
    total = fold_rims(summed)
    return object_field - STEP_SIZE * total


def solution(mesh):
    in_specs = (
        P(None, "row", "col"),
        P("mode", None, None),
        P("mode", None, None),
        P("row", "col", None, None, None),
        P("row", "col", None, None),
        P("row", "col"),
    )
    out_specs = P(None, "row", "col")
    return jax.shard_map(
        per_device, mesh=mesh, in_specs=in_specs, out_specs=out_specs, check_vma=False
    )
```

profile of v0, /device:TPU:1, one launch (start us, length us, event | category | flops | bytes accessed | tf_op | source)
XLA Modules:
  0.0 185.5 jit_solution(7516222423846577421)
XLA Ops:
  6.5 1.0 fusion.137
  7.5 3.9 %collective-permute-start = (f32[2,64,256]{2,1,0:T(8,128)S(1)}, f32[2,64,256]{2,1,0:T(8,128)S(1)}, u32[]{:S(2)}, u32[]{:S(2)}) collective-permute-start(f32[2,64,256]{2,1,0:T(8,128)S(1)} %get-tuple-element.375), channel_id=1, source_target_pairs={{0,16},{1,17},{2,18},{3,19},{4,20},{5,21},{6,22},{7,23},{8,24},{9,... | collective-permute-start | bytes 393224 | tf_op jit(solution)/shard_map/ppermute | solution.py:21
  11.5 1.3 collective-permute-start.1
  12.8 0.9 collective-permute-done
  13.6 1.1 constant_dynamic-update-slice_fusion.1
  14.8 2.4 %collective-permute-done.1 = f32[2,64,256]{2,1,0:T(8,128)S(1)} collective-permute-done((f32[2,64,256]{2,1,0:T(8,128)S(1)}, f32[2,64,256]{2,1,0:T(8,128)S(1)}, u32[]{:S(2)}, u32[]{:S(2)}) %collective-permute-start.1) | collective-permute-done | bytes 131104 | tf_op jit(solution)/shard_map/ppermute | solution.py:23
  17.4 5.1 %collective-permute-start.2 = (f32[2,384,64]{2,1,0:T(8,128)S(1)}, f32[2,384,64]{2,1,0:T(8,128)S(1)}, u32[]{:S(2)}, u32[]{:S(2)}) collective-permute-start(f32[2,384,64]{2,1,0:T(8,128)S(1)} %get-tuple-element.372), channel_id=1, source_target_pairs={{0,4},{4,8},{8,12},{1,5},{5,9},{9,13},{2,6},{6,10},{10,14},{3,7},{... | collective-permute-start | bytes 589832 | tf_op jit(solution)/shard_map/ppermute | solution.py:21
  22.5 1.9 %collective-permute-start.3 = (f32[2,384,64]{2,1,0:T(8,128)S(1)}, f32[2,384,64]{2,1,0:T(8,128)S(1)}, u32[]{:S(2)}, u32[]{:S(2)}) collective-permute-start(f32[2,384,64]{2,1,0:T(8,128)S(1)} %get-tuple-element.373), channel_id=1, source_target_pairs={{4,0},{8,4},{12,8},{5,1},{9,5},{13,9},{6,2},{10,6},{14,10},{7,3},{... | collective-permute-start | bytes 589832 | tf_op jit(solution)/shard_map/ppermute | solution.py:23
  24.5 12.1 %all_gather.6 = f32[4,128,128]{2,1,0:T(8,128)S(1)} all-gather(f32[1,128,128]{2,1,0:T(8,128)S(1)} %copy-done.3), channel_id=1, replica_groups=mesh['row'=2,'col'=4,'mode'=4] {'mode'}, dimensions={0}, use_global_device_ids=true | all-gather | bytes 327680 | tf_op jit(solution)/shard_map/all_gather | solution.py:101
  36.5 12.3 %all_gather.7 = f32[4,128,128]{2,1,0:T(8,128)S(1)} all-gather(f32[1,128,128]{2,1,0:T(8,128)S(1)} %copy-done.4), channel_id=1, replica_groups=mesh['row'=2,'col'=4,'mode'=4] {'mode'}, dimensions={0}, use_global_device_ids=true | all-gather | bytes 327680 | tf_op jit(solution)/shard_map/all_gather | solution.py:102
  50.0 40.9 %while.19 = (s32[]{:T(128)}, f32[2,384,384]{2,1,0:T(8,128)S(1)}, s32[]{:T(128)}, s32[8,2]{0,1:T(2,128)S(1)}, f32[2,384,384]{2,1,0:T(8,128)S(1)}, /*index=5*/f32[...) while((s32[]{:T(128)}, f32[2,384,384]{2,1,0:T(8,128)S(1)}, ...), condition=%wide.region_3.4_spmd.clone.clone, body=%wide.region_0.3_spmd.clone.clone.sunk | while | flops 1617362944 | bytes 15466841 | solution.py:116
  54.9 0.8 fusion.219
  57.2 0.8 fusion.216
  60.9 0.9 fusion.222
  67.9 2.5 %dynamic_update_slice.10 = f32[2,384,384]{2,1,0:T(8,128)S(1)} dynamic-update-slice(f32[2,384,384]{2,1,0:T(8,128)S(1)} %get-tuple-element.463, f32[2,128,128]{2,1,0:T(8,128)S(1)} %multiply_add_fusion.9, s32[]{:T(128)} %constant.176.clone.1..sunk, s32[]{:T(128)S(6)} %select_n.178, s32[]{:T(128)S(6)} %select_n.179) | dynamic-update-slice | bytes 262148 | tf_op jit(solution)/shard_map/while/body/eval_jaxpr/dynamic_update_slice | solution.py:97
  75.3 0.8 fusion.219
  81.4 0.9 fusion.222
  88.3 2.5 %dynamic_update_slice.10 = f32[2,384,384]{2,1,0:T(8,128)S(1)} dynamic-update-slice(f32[2,384,384]{2,1,0:T(8,128)S(1)} %get-tuple-element.463, f32[2,128,128]{2,1,0:T(8,128)S(1)} %multiply_add_fusion.9, s32[]{:T(128)} %constant.176.clone.1..sunk, s32[]{:T(128)S(6)} %select_n.178, s32[]{:T(128)S(6)} %select_n.179) | dynamic-update-slice | bytes 262148 | tf_op jit(solution)/shard_map/while/body/eval_jaxpr/dynamic_update_slice | solution.py:97
  90.9 1.0 copy-done
  91.9 59.9 %all-reduce.2.cloned.1.call-done = f32[2,384,384]{2,1,0:T(8,128)} async-done(((f32[2,384,384]{2,1,0:T(8,128)}), f32[2,384,384]{2,1,0:T(8,128)}) %all-reduce.2.cloned.1.call-update) | async-done | bytes 1179664 | tf_op jit(solution)/shard_map/psum | solution.py:117
  151.8 1.2 fusion.134
  153.0 3.1 %collective-permute-start.4 = (f32[2,64,384]{2,1,0:T(8,128)S(1)}, f32[2,64,384]{2,1,0:T(8,128)S(1)}, u32[]{:S(2)}, u32[]{:S(2)}) collective-permute-start(f32[2,64,384]{2,1,0:T(8,128)S(1)} %get-tuple-element.369), channel_id=1, source_target_pairs={{0,16},{1,17},{2,18},{3,19},{4,20},{5,21},{6,22},{7,23},{8,24},{9,... | collective-permute-start | bytes 589832 | tf_op jit(solution)/shard_map/ppermute | solution.py:21
  156.1 1.3 collective-permute-start.5
  157.4 2.4 %collective-permute-done.4 = f32[2,64,384]{2,1,0:T(8,128)S(1)} collective-permute-done((f32[2,64,384]{2,1,0:T(8,128)S(1)}, f32[2,64,384]{2,1,0:T(8,128)S(1)}, u32[]{:S(2)}, u32[]{:S(2)}) %collective-permute-start.4) | collective-permute-done | bytes 196640 | tf_op jit(solution)/shard_map/ppermute | solution.py:21
  159.8 3.8 %collective-permute-done.5 = f32[2,64,384]{2,1,0:T(8,128)S(1)} collective-permute-done((f32[2,64,384]{2,1,0:T(8,128)S(1)}, f32[2,64,384]{2,1,0:T(8,128)S(1)}, u32[]{:S(2)}, u32[]{:S(2)}) %collective-permute-start.5) | collective-permute-done | bytes 196640 | tf_op jit(solution)/shard_map/ppermute | solution.py:23
  163.8 4.7 %collective-permute-start.6 = (f32[2,256,64]{2,1,0:T(8,128)S(1)}, f32[2,256,64]{2,1,0:T(8,128)S(1)}, u32[]{:S(2)}, u32[]{:S(2)}) collective-permute-start(f32[2,256,64]{2,1,0:T(8,128)S(1)} %get-tuple-element.371), channel_id=1, source_target_pairs={{0,4},{4,8},{8,12},{1,5},{5,9},{9,13},{2,6},{6,10},{10,14},{3,7},{... | collective-permute-start | bytes 393224 | tf_op jit(solution)/shard_map/ppermute | solution.py:21
  168.7 2.1 %collective-permute-start.7 = (f32[2,256,64]{2,1,0:T(8,128)S(1)}, f32[2,256,64]{2,1,0:T(8,128)S(1)}, u32[]{:S(2)}, u32[]{:S(2)}) collective-permute-start(f32[2,256,64]{2,1,0:T(8,128)S(1)} %get-tuple-element.370), channel_id=1, source_target_pairs={{4,0},{8,4},{12,8},{5,1},{9,5},{13,9},{6,2},{10,6},{14,10},{7,3},{... | collective-permute-start | bytes 393224 | tf_op jit(solution)/shard_map/ppermute | solution.py:23
  170.7 1.0 collective-permute-done.6
  171.9 1.1 scatter-add.16
  173.0 3.5 %collective-permute-done.7 = f32[2,256,64]{2,1,0:T(8,128)S(1)} collective-permute-done((f32[2,256,64]{2,1,0:T(8,128)S(1)}, f32[2,256,64]{2,1,0:T(8,128)S(1)}, u32[]{:S(2)}, u32[]{:S(2)}) %collective-permute-start.7) | collective-permute-done | bytes 131104 | tf_op jit(solution)/shard_map/ppermute | solution.py:23
  176.6 1.2 scatter-add.19
  177.8 0.9 multiply_subtract_fusion.3
  (65 shorter events, 25.1 us)
Async XLA Ops:
  6.5 145.2 %all-reduce.2.cloned.1.call-start = ((), (), s32[]{:S(2)}) async-start(), calls=%async_computation | async-start | bytes 2359296 | tf_op jit(solution)/shard_map/psum | solution.py:117
  7.5 6.1 %collective-permute-start = (f32[2,64,256]{2,1,0:T(8,128)S(1)}, f32[2,64,256]{2,1,0:T(8,128)S(1)}, u32[]{:S(2)}, u32[]{:S(2)}) collective-permute-start(f32[2,64,256]{2,1,0:T(8,128)S(1)} %get-tuple-element.375), channel_id=1, source_target_pairs={{0,16},{1,17},{2,18},{3,19},{4,20},{5,21},{6,22},{7,23},{8,24},{9,... | collective-permute-start | bytes 393224 | tf_op jit(solution)/shard_map/ppermute | solution.py:21
  11.5 5.7 %collective-permute-start.1 = (f32[2,64,256]{2,1,0:T(8,128)S(1)}, f32[2,64,256]{2,1,0:T(8,128)S(1)}, u32[]{:S(2)}, u32[]{:S(2)}) collective-permute-start(f32[2,64,256]{2,1,0:T(8,128)S(1)} %get-tuple-element.374), channel_id=1, source_target_pairs={{16,0},{17,1},{18,2},{19,3},{20,4},{21,5},{22,6},{23,7},{24,8},{25... | collective-permute-start | bytes 393224 | tf_op jit(solution)/shard_map/ppermute | solution.py:23
  14.7 9.7 %copy-start.3 = (f32[1,128,128]{2,1,0:T(8,128)S(1)}, f32[1,128,128]{2,1,0:T(8,128)}, u32[]{:S(2)}) copy-start(f32[1,128,128]{2,1,0:T(8,128)} %param.17) | copy-start | bytes 196612
  14.7 21.8 %copy-start.4 = (f32[1,128,128]{2,1,0:T(8,128)S(1)}, f32[1,128,128]{2,1,0:T(8,128)}, u32[]{:S(2)}) copy-start(f32[1,128,128]{2,1,0:T(8,128)} %param.18) | copy-start | bytes 196612
  17.4 31.4 %collective-permute-start.2 = (f32[2,384,64]{2,1,0:T(8,128)S(1)}, f32[2,384,64]{2,1,0:T(8,128)S(1)}, u32[]{:S(2)}, u32[]{:S(2)}) collective-permute-start(f32[2,384,64]{2,1,0:T(8,128)S(1)} %get-tuple-element.372), channel_id=1, source_target_pairs={{0,4},{4,8},{8,12},{1,5},{5,9},{9,13},{2,6},{6,10},{10,14},{3,7},{... | collective-permute-start | bytes 589832 | tf_op jit(solution)/shard_map/ppermute | solution.py:21
  22.5 26.3 %collective-permute-start.3 = (f32[2,384,64]{2,1,0:T(8,128)S(1)}, f32[2,384,64]{2,1,0:T(8,128)S(1)}, u32[]{:S(2)}, u32[]{:S(2)}) collective-permute-start(f32[2,384,64]{2,1,0:T(8,128)S(1)} %get-tuple-element.373), channel_id=1, source_target_pairs={{4,0},{8,4},{12,8},{5,1},{9,5},{13,9},{6,2},{10,6},{14,10},{7,3},{... | collective-permute-start | bytes 589832 | tf_op jit(solution)/shard_map/ppermute | solution.py:23
  49.3 0.7 copy-start.5
  90.9 1.0 copy-start
  151.8 8.0 %copy-start.1 = (f32[2,384,384]{2,1,0:T(8,128)S(1)}, f32[2,384,384]{2,1,0:T(8,128)}, u32[]{:S(2)}) copy-start(f32[2,384,384]{2,1,0:T(8,128)} %all-reduce.2.cloned.1.call-done) | copy-start | bytes 3538948
  151.8 8.0 %slice-start = ((f32[2,384,384]{2,1,0:T(8,128)}), f32[2,256,384]{2,1,0:T(8,128)S(1)}, s32[]{:S(2)}) async-start(f32[2,384,384]{2,1,0:T(8,128)} %all-reduce.2.cloned.1.call-done), calls=%async_computation.1 | async-start | bytes 1572864 | tf_op jit(solution)/shard_map/slice | solution.py:69
  153.0 6.8 %collective-permute-start.4 = (f32[2,64,384]{2,1,0:T(8,128)S(1)}, f32[2,64,384]{2,1,0:T(8,128)S(1)}, u32[]{:S(2)}, u32[]{:S(2)}) collective-permute-start(f32[2,64,384]{2,1,0:T(8,128)S(1)} %get-tuple-element.369), channel_id=1, source_target_pairs={{0,16},{1,17},{2,18},{3,19},{4,20},{5,21},{6,22},{7,23},{8,24},{9,... | collective-permute-start | bytes 589832 | tf_op jit(solution)/shard_map/ppermute | solution.py:21
  156.1 7.5 %collective-permute-start.5 = (f32[2,64,384]{2,1,0:T(8,128)S(1)}, f32[2,64,384]{2,1,0:T(8,128)S(1)}, u32[]{:S(2)}, u32[]{:S(2)}) collective-permute-start(f32[2,64,384]{2,1,0:T(8,128)S(1)} %get-tuple-element.368), channel_id=1, source_target_pairs={{16,0},{17,1},{18,2},{19,3},{20,4},{21,5},{22,6},{23,7},{24,8},{25... | collective-permute-start | bytes 589832 | tf_op jit(solution)/shard_map/ppermute | solution.py:23
  163.8 8.0 %collective-permute-start.6 = (f32[2,256,64]{2,1,0:T(8,128)S(1)}, f32[2,256,64]{2,1,0:T(8,128)S(1)}, u32[]{:S(2)}, u32[]{:S(2)}) collective-permute-start(f32[2,256,64]{2,1,0:T(8,128)S(1)} %get-tuple-element.371), channel_id=1, source_target_pairs={{0,4},{4,8},{8,12},{1,5},{5,9},{9,13},{2,6},{6,10},{10,14},{3,7},{... | collective-permute-start | bytes 393224 | tf_op jit(solution)/shard_map/ppermute | solution.py:21
  168.7 9.2 %copy-start.2 = (f32[2,256,256]{2,1,0:T(8,128)S(1)}, f32[2,256,256]{2,1,0:T(8,128)}, u32[]{:S(2)}) copy-start(f32[2,256,256]{2,1,0:T(8,128)} %param.16) | copy-start | bytes 1572868
  168.7 7.8 %collective-permute-start.7 = (f32[2,256,64]{2,1,0:T(8,128)S(1)}, f32[2,256,64]{2,1,0:T(8,128)S(1)}, u32[]{:S(2)}, u32[]{:S(2)}) collective-permute-start(f32[2,256,64]{2,1,0:T(8,128)S(1)} %get-tuple-element.370), channel_id=1, source_target_pairs={{4,0},{8,4},{12,8},{5,1},{9,5},{13,9},{6,2},{10,6},{14,10},{7,3},{... | collective-permute-start | bytes 393224 | tf_op jit(solution)/shard_map/ppermute | solution.py:23
Sparse Core Ops, SparseCore 0:
  92.0 59.7 all-reduce.1
where the time goes:
time: 186 us
  waiting for transfers between devices  73.9 us (40%)
  blocking collectives  24.4 us (13%)
  matrix products  23.7 us (13%)
  starting transfers between devices  23.4 us (13%)
  local copies, waits for them, and re-layouts  14.2 us (8%)
  between operations  13.6 us (7%)
  loops' own time  8.74 us (5%)
  other arithmetic  3.71 us (2%)
    psum x1, waiting for transfers between devices, per_device(): summed = lax.psum(gradient, 'mode')  59.9 us
    ppermute x4, starting transfers between devices, padded(): lax.ppermute(tail, axis, [(i, (i + 1) % count) for i in range(ends)])  16.9 us
    all_gather x1, blocking collectives, per_device(): lax.all_gather(probe_imag, 'mode', axis=0, tiled=True)  12.3 us
    all_gather x1, blocking collectives, per_device(): lax.all_gather(probe_real, 'mode', axis=0, tiled=True)  12.1 us
    ppermute x4, waiting for transfers between devices, padded(): lax.ppermute(head, axis, [((i + 1) % count, i) for i in range(ends)])  9.72 us
    another operation x1, loops' own time, per_device(): gradient = lax.fori_loop(0, SLOTS // group, advance_own, gradient)  8.74 us
    ppermute x4, starting transfers between devices, padded(): lax.ppermute(head, axis, [((i + 1) % count, i) for i in range(ends)])  6.56 us
    dynamic_update_slice x2, local copies, waits for them, and re-layouts, deposit(): lax.dynamic_update_slice(gradient, previous + contrib * weight, corner)  4.99 us
  transfers between devices with their start and end apart: 9, of which 7 were waited for; matrix products, arithmetic and copies ran while one was open for 1% of the time, Pallas kernels for 0%

commit v1 on v0

--- a/solution.py
+++ b/solution.py
@@ -114,7 +114,7 @@
         return deposit(gradient, slot, jnp.sum(terms, axis=0))
 
     gradient = lax.fori_loop(0, SLOTS // group, advance_own, gradient)
-    summed = lax.psum(gradient, "mode")
+    summed = jnp.sum(lax.all_gather(gradient, "mode"), axis=0)
     total = fold_rims(summed)
     return object_field - STEP_SIZE * total
 

time: 186 us -> 222 us (1.19)
  waiting for transfers between devices: 73.9 us -> 107 us
  other arithmetic: 3.71 us -> 6.43 us
    all_gather x0 -> x1, waiting for transfers between devices: none -> 93.1 us  [per_device(): summed = jnp.sum(lax.all_gather(gradient, 'mode'), axis=0)]
    psum x1 -> x0, waiting for transfers between devices: 59.9 us -> none  [per_device(): summed = lax.psum(gradient, 'mode')]
    reduce_sum x0 -> x1, other arithmetic: none -> 2.72 us  [per_device(): summed = jnp.sum(lax.all_gather(gradient, 'mode'), axis=0)]
where the time goes in v1:
time: 222 us; the launch traced here: 221 us
  waiting for transfers between devices  107 us (48%)
  blocking collectives  24.4 us (11%)
  matrix products  23.7 us (11%)
  starting transfers between devices  23.6 us (11%)
  between operations  13.6 us (6%)
  local copies, waits for them, and re-layouts  13.2 us (6%)
  loops' own time  9.21 us (4%)
  other arithmetic  6.43 us (3%)
    all_gather x1, waiting for transfers between devices, per_device(): summed = jnp.sum(lax.all_gather(gradient, 'mode'), axis=0)  93.1 us
    ppermute x4, starting transfers between devices, padded(): lax.ppermute(tail, axis, [(i, (i + 1) % count) for i in range(ends)])  17 us
    all_gather x1, blocking collectives, per_device(): lax.all_gather(probe_imag, 'mode', axis=0, tiled=True)  12.3 us
    all_gather x1, blocking collectives, per_device(): lax.all_gather(probe_real, 'mode', axis=0, tiled=True)  12.1 us
    ppermute x4, waiting for transfers between devices, padded(): lax.ppermute(head, axis, [((i + 1) % count, i) for i in range(ends)])  9.79 us
    another operation x1, loops' own time, per_device(): gradient = lax.fori_loop(0, SLOTS // group, advance_own, gradient)  9.21 us
    ppermute x4, starting transfers between devices, padded(): lax.ppermute(head, axis, [((i + 1) % count, i) for i in range(ends)])  6.56 us
    dynamic_update_slice x2, local copies, waits for them, and re-layouts, deposit(): lax.dynamic_update_slice(gradient, previous + contrib * weight, corner)  4.99 us
  transfers between devices with their start and end apart: 9, of which 7 were waited for; matrix products, arithmetic and copies ran while one was open for 1% of the time, Pallas kernels for 0%

profile of v1, /device:TPU:1, one launch (start us, length us, event | category | flops | bytes accessed | tf_op | source)
XLA Modules:
  0.0 221.0 jit_solution(14610608037648612115)
XLA Ops:
  6.5 1.0 fusion.137
  7.5 3.9 %collective-permute-start = (f32[2,64,256]{2,1,0:T(8,128)S(1)}, f32[2,64,256]{2,1,0:T(8,128)S(1)}, u32[]{:S(2)}, u32[]{:S(2)}) collective-permute-start(f32[2,64,256]{2,1,0:T(8,128)S(1)} %get-tuple-element.375), channel_id=1, source_target_pairs={{0,16},{1,17},{2,18},{3,19},{4,20},{5,21},{6,22},{7,23},{8,24},{9,... | collective-permute-start | bytes 393224 | tf_op jit(solution)/shard_map/ppermute | solution.py:21
  11.5 1.3 collective-permute-start.1
  12.8 0.9 collective-permute-done
  13.6 1.1 constant_dynamic-update-slice_fusion.1
  14.8 2.4 %collective-permute-done.1 = f32[2,64,256]{2,1,0:T(8,128)S(1)} collective-permute-done((f32[2,64,256]{2,1,0:T(8,128)S(1)}, f32[2,64,256]{2,1,0:T(8,128)S(1)}, u32[]{:S(2)}, u32[]{:S(2)}) %collective-permute-start.1) | collective-permute-done | bytes 131104 | tf_op jit(solution)/shard_map/ppermute | solution.py:23
  17.4 5.1 %collective-permute-start.2 = (f32[2,384,64]{2,1,0:T(8,128)S(1)}, f32[2,384,64]{2,1,0:T(8,128)S(1)}, u32[]{:S(2)}, u32[]{:S(2)}) collective-permute-start(f32[2,384,64]{2,1,0:T(8,128)S(1)} %get-tuple-element.372), channel_id=1, source_target_pairs={{0,4},{4,8},{8,12},{1,5},{5,9},{9,13},{2,6},{6,10},{10,14},{3,7},{... | collective-permute-start | bytes 589832 | tf_op jit(solution)/shard_map/ppermute | solution.py:21
  22.5 1.9 collective-permute-start.3
  24.5 12.1 %all_gather.12 = f32[4,128,128]{2,1,0:T(8,128)S(1)} all-gather(f32[1,128,128]{2,1,0:T(8,128)S(1)} %copy-done.2), channel_id=1, replica_groups=mesh['row'=2,'col'=4,'mode'=4] {'mode'}, dimensions={0}, use_global_device_ids=true | all-gather | bytes 327680 | tf_op jit(solution)/shard_map/all_gather | solution.py:101
  36.5 12.3 %all_gather.13 = f32[4,128,128]{2,1,0:T(8,128)S(1)} all-gather(f32[1,128,128]{2,1,0:T(8,128)S(1)} %copy-done.3), channel_id=1, replica_groups=mesh['row'=2,'col'=4,'mode'=4] {'mode'}, dimensions={0}, use_global_device_ids=true | all-gather | bytes 327680 | tf_op jit(solution)/shard_map/all_gather | solution.py:102
  50.0 41.5 %while.19 = (s32[]{:T(128)}, f32[2,384,384]{2,1,0:T(8,128)S(1)}, s32[]{:T(128)}, s32[8,2]{0,1:T(2,128)S(1)}, f32[2,384,384]{2,1,0:T(8,128)S(1)}, /*index=5*/f32[...) while((s32[]{:T(128)}, f32[2,384,384]{2,1,0:T(8,128)S(1)}, ...), condition=%wide.region_3.4_spmd.clone.clone, body=%wide.region_0.3_spmd.clone.clone.sunk | while | flops 1617362944 | bytes 15466841 | solution.py:116
  55.1 0.8 fusion.219
  61.1 0.9 fusion.222
  68.1 2.5 %dynamic_update_slice.10 = f32[2,384,384]{2,1,0:T(8,128)S(1)} dynamic-update-slice(f32[2,384,384]{2,1,0:T(8,128)S(1)} %get-tuple-element.463, f32[2,128,128]{2,1,0:T(8,128)S(1)} %multiply_add_fusion.9, s32[]{:T(128)} %constant.177.clone.1..sunk, s32[]{:T(128)S(6)} %select_n.178, s32[]{:T(128)S(6)} %select_n.179) | dynamic-update-slice | bytes 262148 | tf_op jit(solution)/shard_map/while/body/eval_jaxpr/dynamic_update_slice | solution.py:97
  75.8 0.8 fusion.219
  78.0 0.8 fusion.216
  81.8 0.9 fusion.222
  88.8 2.5 %dynamic_update_slice.10 = f32[2,384,384]{2,1,0:T(8,128)S(1)} dynamic-update-slice(f32[2,384,384]{2,1,0:T(8,128)S(1)} %get-tuple-element.463, f32[2,128,128]{2,1,0:T(8,128)S(1)} %multiply_add_fusion.9, s32[]{:T(128)} %constant.177.clone.1..sunk, s32[]{:T(128)S(6)} %select_n.178, s32[]{:T(128)S(6)} %select_n.179) | dynamic-update-slice | bytes 262148 | tf_op jit(solution)/shard_map/while/body/eval_jaxpr/dynamic_update_slice | solution.py:97
  91.5 1.0 copy-done
  92.5 93.1 %all-gather.3.cloned.1.call-done = f32[8,384,384]{2,1,0:T(8,128)} async-done(((f32[2,384,384]{2,1,0:T(8,128)}), f32[8,384,384]{2,1,0:T(8,128)}) %all-gather.3.cloned.1.call-update) | async-done | bytes 4718608 | tf_op jit(solution)/shard_map/all_gather | solution.py:117
  185.7 2.7 %reduce_sum.35 = f32[2,384,384]{2,1,0:T(8,128)S(1)} reduce(f32[4,2,384,384]{3,2,1,0:T(8,128)} %bitcast.144, f32[]{:T(128)} %constant.178.clone.1), dimensions={0}, to_apply=%region_4.5 | reduce | flops 884736 | bytes 5898244 | tf_op jit(solution)/shard_map/reduce_sum | solution.py:117
  188.4 3.1 %collective-permute-start.4 = (f32[2,64,384]{2,1,0:T(8,128)S(1)}, f32[2,64,384]{2,1,0:T(8,128)S(1)}, u32[]{:S(2)}, u32[]{:S(2)}) collective-permute-start(f32[2,64,384]{2,1,0:T(8,128)S(1)} %get-tuple-element.369), channel_id=1, source_target_pairs={{0,16},{1,17},{2,18},{3,19},{4,20},{5,21},{6,22},{7,23},{8,24},{9,... | collective-permute-start | bytes 589832 | tf_op jit(solution)/shard_map/ppermute | solution.py:21
  191.6 1.3 collective-permute-start.5
  192.9 2.1 collective-permute-done.4
  195.0 3.9 %collective-permute-done.5 = f32[2,64,384]{2,1,0:T(8,128)S(1)} collective-permute-done((f32[2,64,384]{2,1,0:T(8,128)S(1)}, f32[2,64,384]{2,1,0:T(8,128)S(1)}, u32[]{:S(2)}, u32[]{:S(2)}) %collective-permute-start.5) | collective-permute-done | bytes 196640 | tf_op jit(solution)/shard_map/ppermute | solution.py:23
  199.1 4.9 %collective-permute-start.6 = (f32[2,256,64]{2,1,0:T(8,128)S(1)}, f32[2,256,64]{2,1,0:T(8,128)S(1)}, u32[]{:S(2)}, u32[]{:S(2)}) collective-permute-start(f32[2,256,64]{2,1,0:T(8,128)S(1)} %get-tuple-element.371), channel_id=1, source_target_pairs={{0,4},{4,8},{8,12},{1,5},{5,9},{9,13},{2,6},{6,10},{10,14},{3,7},{... | collective-permute-start | bytes 393224 | tf_op jit(solution)/shard_map/ppermute | solution.py:21
  204.2 2.1 collective-permute-start.7
  206.2 1.0 collective-permute-done.6
  207.4 1.1 scatter-add.16
  208.5 3.5 %collective-permute-done.7 = f32[2,256,64]{2,1,0:T(8,128)S(1)} collective-permute-done((f32[2,256,64]{2,1,0:T(8,128)S(1)}, f32[2,256,64]{2,1,0:T(8,128)S(1)}, u32[]{:S(2)}, u32[]{:S(2)}) %collective-permute-start.7) | collective-permute-done | bytes 131104 | tf_op jit(solution)/shard_map/ppermute | solution.py:23
  212.1 1.2 scatter-add.19
  213.3 0.9 multiply_subtract_fusion.3
  (63 shorter events, 25.3 us)
Async XLA Ops:
  6.5 179.1 %all-gather.3.cloned.1.call-start = ((), (), s32[]{:S(2)}) async-start(), calls=%async_computation | async-start | bytes 5898240 | tf_op jit(solution)/shard_map/all_gather | solution.py:117
  7.5 6.1 %collective-permute-start = (f32[2,64,256]{2,1,0:T(8,128)S(1)}, f32[2,64,256]{2,1,0:T(8,128)S(1)}, u32[]{:S(2)}, u32[]{:S(2)}) collective-permute-start(f32[2,64,256]{2,1,0:T(8,128)S(1)} %get-tuple-element.375), channel_id=1, source_target_pairs={{0,16},{1,17},{2,18},{3,19},{4,20},{5,21},{6,22},{7,23},{8,24},{9,... | collective-permute-start | bytes 393224 | tf_op jit(solution)/shard_map/ppermute | solution.py:21
  11.5 5.7 %collective-permute-start.1 = (f32[2,64,256]{2,1,0:T(8,128)S(1)}, f32[2,64,256]{2,1,0:T(8,128)S(1)}, u32[]{:S(2)}, u32[]{:S(2)}) collective-permute-start(f32[2,64,256]{2,1,0:T(8,128)S(1)} %get-tuple-element.374), channel_id=1, source_target_pairs={{16,0},{17,1},{18,2},{19,3},{20,4},{21,5},{22,6},{23,7},{24,8},{25... | collective-permute-start | bytes 393224 | tf_op jit(solution)/shard_map/ppermute | solution.py:23
  14.7 9.7 %copy-start.2 = (f32[1,128,128]{2,1,0:T(8,128)S(1)}, f32[1,128,128]{2,1,0:T(8,128)}, u32[]{:S(2)}) copy-start(f32[1,128,128]{2,1,0:T(8,128)} %param.17) | copy-start | bytes 196612
  14.7 21.8 %copy-start.3 = (f32[1,128,128]{2,1,0:T(8,128)S(1)}, f32[1,128,128]{2,1,0:T(8,128)}, u32[]{:S(2)}) copy-start(f32[1,128,128]{2,1,0:T(8,128)} %param.18) | copy-start | bytes 196612
  17.4 31.4 %collective-permute-start.2 = (f32[2,384,64]{2,1,0:T(8,128)S(1)}, f32[2,384,64]{2,1,0:T(8,128)S(1)}, u32[]{:S(2)}, u32[]{:S(2)}) collective-permute-start(f32[2,384,64]{2,1,0:T(8,128)S(1)} %get-tuple-element.372), channel_id=1, source_target_pairs={{0,4},{4,8},{8,12},{1,5},{5,9},{9,13},{2,6},{6,10},{10,14},{3,7},{... | collective-permute-start | bytes 589832 | tf_op jit(solution)/shard_map/ppermute | solution.py:21
  22.5 26.3 %collective-permute-start.3 = (f32[2,384,64]{2,1,0:T(8,128)S(1)}, f32[2,384,64]{2,1,0:T(8,128)S(1)}, u32[]{:S(2)}, u32[]{:S(2)}) collective-permute-start(f32[2,384,64]{2,1,0:T(8,128)S(1)} %get-tuple-element.373), channel_id=1, source_target_pairs={{4,0},{8,4},{12,8},{5,1},{9,5},{13,9},{6,2},{10,6},{14,10},{7,3},{... | collective-permute-start | bytes 589832 | tf_op jit(solution)/shard_map/ppermute | solution.py:23
  49.3 0.7 copy-start.4
  91.5 1.0 copy-start
  188.4 6.6 %collective-permute-start.4 = (f32[2,64,384]{2,1,0:T(8,128)S(1)}, f32[2,64,384]{2,1,0:T(8,128)S(1)}, u32[]{:S(2)}, u32[]{:S(2)}) collective-permute-start(f32[2,64,384]{2,1,0:T(8,128)S(1)} %get-tuple-element.369), channel_id=1, source_target_pairs={{0,16},{1,17},{2,18},{3,19},{4,20},{5,21},{6,22},{7,23},{8,24},{9,... | collective-permute-start | bytes 589832 | tf_op jit(solution)/shard_map/ppermute | solution.py:21
  191.6 7.3 %collective-permute-start.5 = (f32[2,64,384]{2,1,0:T(8,128)S(1)}, f32[2,64,384]{2,1,0:T(8,128)S(1)}, u32[]{:S(2)}, u32[]{:S(2)}) collective-permute-start(f32[2,64,384]{2,1,0:T(8,128)S(1)} %get-tuple-element.368), channel_id=1, source_target_pairs={{16,0},{17,1},{18,2},{19,3},{20,4},{21,5},{22,6},{23,7},{24,8},{25... | collective-permute-start | bytes 589832 | tf_op jit(solution)/shard_map/ppermute | solution.py:23
  199.1 8.2 %collective-permute-start.6 = (f32[2,256,64]{2,1,0:T(8,128)S(1)}, f32[2,256,64]{2,1,0:T(8,128)S(1)}, u32[]{:S(2)}, u32[]{:S(2)}) collective-permute-start(f32[2,256,64]{2,1,0:T(8,128)S(1)} %get-tuple-element.371), channel_id=1, source_target_pairs={{0,4},{4,8},{8,12},{1,5},{5,9},{9,13},{2,6},{6,10},{10,14},{3,7},{... | collective-permute-start | bytes 393224 | tf_op jit(solution)/shard_map/ppermute | solution.py:21
  204.2 9.2 %copy-start.1 = (f32[2,256,256]{2,1,0:T(8,128)S(1)}, f32[2,256,256]{2,1,0:T(8,128)}, u32[]{:S(2)}) copy-start(f32[2,256,256]{2,1,0:T(8,128)} %param.16) | copy-start | bytes 1572868
  204.2 7.8 %collective-permute-start.7 = (f32[2,256,64]{2,1,0:T(8,128)S(1)}, f32[2,256,64]{2,1,0:T(8,128)S(1)}, u32[]{:S(2)}, u32[]{:S(2)}) collective-permute-start(f32[2,256,64]{2,1,0:T(8,128)S(1)} %get-tuple-element.370), channel_id=1, source_target_pairs={{4,0},{8,4},{12,8},{5,1},{9,5},{13,9},{6,2},{10,6},{14,10},{7,3},{... | collective-permute-start | bytes 393224 | tf_op jit(solution)/shard_map/ppermute | solution.py:23
Sparse Core Ops, SparseCore 0:
  92.6 92.9 all-gather.2
